TPU v7x, 256 devices: a whole 4x4x8 slice. The times are simulated.
256 devices in a mesh: depth: 64 (over z, y, core), tile: 4 (over x).
Axes of the slice: x: 4, y: 4, z: 8, core: 2. Of those that a mesh axis runs over, the one named last changes fastest.
Arguments:
- volume: bfloat16 [768, 4, 768, 512], P('depth', 'tile'), may hold values from -6 to 6
- table_index: int32 [768, 4, 768, 32], P('depth', 'tile'), may hold values from 0 to 15
- brick_position: int32 [64], replicated, may hold values from 0 to 63, each once
- tf_center: float32 [16], replicated, may hold values from -1.5 to 1.5
- tf_width: float32 [16], replicated, may hold values from 0.3 to 1.2
- tf_peak: float32 [16], replicated, may hold values from 2 to 32
- tf_color: float32 [3, 16], replicated, may hold values from 0.1 to 1
Outputs:
- frame: float32 [4, 4, 768, 512], P(None, 'tile', 'depth')
Inputs may be any that keep to these rules, and one draw needn't show every extreme that they name: `brick_position`: each depth rank has a different position.
All inputs are finite; a program needn't handle non-finite values.
Results may differ from a plain program's by a relative error of at most 0.0003.
Values may be sent and summed in bfloat16 or wider, within the bound.
No kernel may reach another device: no remote copies, remote signals or barrier semaphores. Data moves between devices by JAX's collectives and lax.ppermute only.
A program may use at most 128 MiB of HBM per device.

v0:
```python
import functools

import jax
import jax.numpy as jnp
from jax import lax
from jax.experimental import pallas as pl
from jax.experimental.pallas import tpu as pltpu
from jax.sharding import PartitionSpec as P


CELL = 16
LANES = 128
SIDE = 8
BAND = 256
LOG2E = 1.4426950408889634
LEVELS = 65535.0
SCALE = LEVELS**4
CHUNKS = ((1,), (0, 2, 3))
EDGES = 8
STRIP = 4
LIGHT = 32
RIMS = LANES
SHADE_GAIN = 0.7 * 0.6 * 0.6
SHADE_BASE = 0.3 / SHADE_GAIN

NN = (((1,), (0,)), ((), ()))


def from_partner(value, axis, apart):
    return lax.ppermute(value, axis, [(i, i ^ 1 << apart) for i in range(lax.axis_size(axis))])


def code(value):
    root = lax.rsqrt(lax.rsqrt(jnp.maximum(value, 0.0)))
    return (root + 0.5).astype(jnp.int32)


def decode(word):
    root = word.astype(jnp.float32) * (1.0 / LEVELS)
    square = root * root
    return square * square


def march_kernel(tiles, spans, sizes, *refs):
    steps, height, width, total = sizes
    middle = len(spans) == 1
    count = len(tiles)
    center_ref, wide_ref, peak_ref, color_ref, vol_ref, rim_ref, index_ref, outer_ref, edge_ref = refs[:9]
    first = outer_ref is None
    out_ref, done_a, done_b = refs[9:12]
    scratch = refs[12:]
    (band_ref, ends_ref, table_ref, left_ref, value_ref, energy_ref, shade_ref, param_ref, pair_a, pair_b, turn_a, turn_b) = scratch[:12]
    part = pl.program_id(0)
    halves = BAND // LANES
    groups = LANES // CELL

    @pl.when(part == 0)
    def _():
        k = lax.broadcasted_iota(jnp.int32, (BAND, BAND), 0)
        r = lax.broadcasted_iota(jnp.int32, (BAND, BAND), 1)
        band_ref[...] = jnp.where(k == r + 1, 1.0, jnp.where(k == r - 1, -1.0, 0.0)).astype(jnp.bfloat16)
        k = lax.broadcasted_iota(jnp.int32, (RIMS, BAND), 0)
        r = lax.broadcasted_iota(jnp.int32, (RIMS, BAND), 1)
        edge = jnp.where(r == 0, -1.0, 0.0), jnp.where(r == BAND - 1, 1.0, 0.0)
        for s in range(steps):
            ends = jnp.where(k == 2 * s, edge[0], jnp.where(k == 2 * s + 1, edge[1], 0.0))
            ends_ref[s] = ends.astype(jnp.bfloat16)
        shape = (8, 16)
        scale = (0.5 * LOG2E) ** 0.5 / wide_ref[...]
        table_ref[0, :, 0:16] = jnp.broadcast_to(center_ref[...], shape)
        table_ref[1, :, 0:16] = jnp.broadcast_to(scale, shape)
        table_ref[2, :, 0:16] = jnp.broadcast_to(jnp.log2(peak_ref[...] * (0.25 * LOG2E / total)), shape)
        for n in range(3):
            table_ref[3 + n, :, 0:16] = jnp.broadcast_to(color_ref[n : n + 1, :] * (SHADE_GAIN * SCALE), shape)
        if first:
            spots_ref = scratch[12]
            col = lax.broadcasted_iota(jnp.int32, (width, LANES), 0)
            lane = lax.broadcasted_iota(jnp.int32, (width, LANES), 1)
            which = lane % EDGES
            want = jnp.where(which == 0, 0, (which + 1) // 2 * LANES - which % 2)
            spots_ref[...] = jnp.where(col == want, 1.0, 0.0).astype(jnp.bfloat16)

    if first:
        spots_ref = scratch[12]
        rows = vol_ref[...].reshape(steps * BAND, width)
        seen = lax.dot_general(rows, spots_ref[...], NN, preferred_element_type=jnp.float32)
        owner = lax.broadcasted_iota(jnp.int32, (BAND, LANES), 1) // EDGES
        found = jnp.zeros((BAND, LANES), jnp.float32)
        for s in range(steps):
            found = jnp.where(owner == s, seen[BAND * s : BAND * s + BAND], found)
        for m in range(halves):
            edge_ref[m] = found[LANES * m : LANES * m + LANES].T

    for k, t in enumerate(tiles):
        rims = rim_ref[:, LANES * t : LANES * t + LANES].T
        for n in range(2):
            left_ref[n, LANES * k : LANES * k + LANES, BAND : BAND + RIMS] = rims[:, 0:RIMS]

    def turn(s):
        for k in range(count):
            t = tiles[k]
            at = slice(k * LANES, k * LANES + LANES)
            source = vol_ref[s, :, LANES * t : LANES * t + LANES] if first else vol_ref[k][s]
            turned = source.T
            left_ref[s % 2, at, 0:BAND] = turned
            for m in range(halves):
                lanes = slice(LANES * m, LANES * m + LANES)
                value_ref[s, k, m, SIDE : SIDE + LANES, :] = turned[:, lanes].astype(jnp.float32)
                if t == 0:
                    before = outer_ref[0, s : s + 1, lanes]
                else:
                    before = edge_ref[m, EDGES * s + 2 * t - 1 : EDGES * s + 2 * t, :]
                if t == width // LANES - 1:
                    after = outer_ref[1, s : s + 1, lanes]
                else:
                    after = edge_ref[m, EDGES * s + 2 * t + 2 : EDGES * s + 2 * t + 3, :]
                value_ref[s, k, m, SIDE - 1 : SIDE, :] = before
                value_ref[s, k, m, SIDE + LANES : SIDE + LANES + 1, :] = after
                index = index_ref[s, groups * t : groups * t + groups, lanes]
                for p in range(6):
                    param_ref[s, p, k * halves + m] = jnp.take_along_axis(table_ref[p], index, axis=1)
        right = jnp.concatenate([band_ref[...], ends_ref[s]], axis=0)
        return lax.dot_general(left_ref[s % 2], right, NN, preferred_element_type=jnp.float32)

    def light(s, grad):
        for k in range(count):
            for m in range(halves):
                lane = k * halves + m
                for c in range(0, LANES, LIGHT):
                    ahead = value_ref[s, k, m, SIDE + 1 + c : SIDE + 1 + c + LIGHT, :]
                    behind = value_ref[s, k, m, SIDE - 1 + c : SIDE - 1 + c + LIGHT, :]
                    grad_x = ahead - behind
                    grad_y = grad[k * LANES + c : k * LANES + c + LIGHT, LANES * m : LANES * m + LANES]
                    energy = grad_x * grad_x + grad_y * grad_y
                    facing = grad_x + (0.8 / 0.6) * grad_y
                    energy_ref[s, lane, c : c + LIGHT, :] = energy
                    shade_ref[s, lane, c : c + LIGHT, :] = SHADE_BASE + facing * facing / (4.0 + energy)

    grad = turn(0)
    for s in range(steps):
        ready = grad
        if s + 1 < steps:
            grad = turn(s + 1)
        light(s, ready)

    def strip(i, carry):
        g = i % (groups // STRIP) * STRIP
        lane = i // (groups // STRIP)
        k = lane // halves
        m = lane % halves
        base = pl.multiple_of(g * CELL, CELL)
        zero = jnp.zeros((8, LANES), jnp.float32)
        state = [[zero, zero + 1.0, zero, zero, zero] for _ in range(2 * STRIP)]
        for s in range(steps):
            for u in range(2 * STRIP):
                if u % 2 == 0:
                    param = [param_ref[s, p, lane, pl.ds(g + u // 2, 8, stride=0), :] for p in range(6)]
                depth, trans, red, green, blue = state[u]
                at = base + 8 * u
                value = value_ref[s, k, m, pl.ds(at + SIDE, 8), :]
                energy = energy_ref[s, lane, pl.ds(at, 8), :]
                shade = shade_ref[s, lane, pl.ds(at, 8), :]
                scaled = (value - param[0]) * param[1]
                rate = jnp.exp2(param[2] - scaled * scaled)
                depth = depth - rate * energy
                after = jnp.exp2(depth)
                weight = (trans - after) * shade
                red = red + weight * param[3]
                green = green + weight * param[4]
                blue = blue + weight * param[5]
                state[u] = [depth, after, red, green, blue]
        for u in range(2 * STRIP):
            depth, trans, red, green, blue = state[u]
            at = pl.ds(base + 8 * u, 8)
            pair_a[lane, at, :] = (code(red) << 16) | code(green)
            pair_b[lane, at, :] = (code(blue) << 16) | code((1.0 - trans) * SCALE)
        return carry

    lax.fori_loop(0, groups // STRIP * count * halves, strip, 0)
    for k in range(count):
        for m in range(halves):
            if middle:
                rows = slice(m * LANES, m * LANES + LANES)
                done_a[k, rows, :] = pair_a[k * halves + m].T
                done_b[k, rows, :] = pair_b[k * halves + m].T
            else:
                row = part * (BAND * (spans[1] - spans[0])) + (BAND * spans[0] + m * LANES)
                rows = pl.ds(pl.multiple_of(row, LANES), LANES)
                turn_a[k, rows, :] = pair_a[k * halves + m].T
                turn_b[k, rows, :] = pair_b[k * halves + m].T
    if middle:
        return

    @pl.when(part == len(spans) - 1)
    def _():
        if done_a is not None:
            turn_a[:, BAND : 2 * BAND, :] = done_a[...]
            turn_b[:, BAND : 2 * BAND, :] = done_b[...]
        piece = height // out_ref.shape[0]

        def pack(d, carry):
            for u in range(4):
                e = d * 4 + u
                r = e * piece
                for k in range(count):
                    lanes = slice(LANES * k, LANES * k + LANES)
                    out_ref[e, 0:8, lanes] = turn_a[k, pl.ds(r, 8), :]
                    out_ref[e, 8:12, lanes] = turn_a[k, pl.ds(r + 8, 4), :]
                    out_ref[e, 12:16, lanes] = turn_b[k, pl.ds(r + 8, 4), :]
                    out_ref[e, 16:24, lanes] = turn_b[k, pl.ds(r, 8), :]
            return carry

        lax.fori_loop(0, out_ref.shape[0] // 4, pack, 0)


def march(tiles, spans, ranks, tables, samples, rim_rows, cells, outer=None, edges=None, done=None):
    steps, height, width = samples.shape
    first = outer is None
    middle = len(spans) == 1
    count = len(tiles)
    halves = BAND // LANES
    at = lambda n: spans[0] + n * (spans[-1] - spans[0]) // max(len(spans) - 1, 1)

    def body(*refs):
        refs = list(refs)
        if not first:
            refs[4 : 4 + count] = [refs[4 : 4 + count]]
            refs[10:10] = [None, None]
        elif middle:
            done_a, done_b, edge = refs[7:10]
            refs[7:10] = [None, edge, None, done_a, done_b]
        else:
            done_a, done_b, out, edge = refs[7:11]
            refs[7:11] = [None, edge, out, done_a, done_b]
        march_kernel(tiles, spans, (steps, height, width, steps * ranks), *refs)

    small = lambda shape: pl.BlockSpec(shape, lambda n: (0,) * len(shape))
    in_specs = [small((1, 16)), small((1, 16)), small((1, 16)), small((3, 16))]
    args = list(tables)
    if first:
        in_specs.append(pl.BlockSpec((steps, BAND, width), lambda n: (0, at(n), 0)))
        args.append(samples)
    else:
        for t in tiles:
            in_specs.append(pl.BlockSpec((steps, BAND, LANES), lambda n, t=t: (0, at(n), t)))
            args.append(samples)
    in_specs += [
        pl.BlockSpec((None, LANES, width), lambda n: (n, 0, 0)),
        pl.BlockSpec((steps, width // CELL, BAND), lambda n: (0, 0, at(n))),
    ]
    args += [rim_rows, cells]
    shape = (ranks, 2 * height // ranks, LANES * count)
    half = (count, BAND, LANES)
    if middle:
        out_shape = [jax.ShapeDtypeStruct(half, jnp.int32)] * 2
        out_specs = [small(half)] * 2
    else:
        out_shape = [jax.ShapeDtypeStruct(shape, jnp.int32)]
        out_specs = [small(shape)]
    scratch = [
        pltpu.VMEM((BAND, BAND), jnp.bfloat16),
        pltpu.VMEM((steps, RIMS, BAND), jnp.bfloat16),
        pltpu.VMEM((6, 8, LANES), jnp.float32),
        pltpu.VMEM((2, count * LANES, BAND + RIMS), jnp.bfloat16),
        pltpu.VMEM((steps, count, halves, LANES + 2 * SIDE, LANES), jnp.float32),
        pltpu.VMEM((steps, count * halves, LANES, LANES), jnp.float32),
        pltpu.VMEM((steps, count * halves, LANES, LANES), jnp.float32),
        pltpu.VMEM((steps, 6, count * halves, LANES // CELL, LANES), jnp.float32),
        pltpu.VMEM((count * halves, LANES, LANES), jnp.int32),
        pltpu.VMEM((count * halves, LANES, LANES), jnp.int32),
        pltpu.VMEM((count, height, LANES), jnp.int32),
        pltpu.VMEM((count, height, LANES), jnp.int32),
    ]
    if first:
        out_shape.append(jax.ShapeDtypeStruct((len(spans) * halves, LANES, LANES), jnp.float32))
        out_specs.append(pl.BlockSpec((halves, LANES, LANES), lambda n: (n, 0, 0)))
        scratch.append(pltpu.VMEM((width, LANES), jnp.bfloat16))
        if done is not None:
            in_specs += [small(half)] * 2
            args += done
    else:
        in_specs.append(pl.BlockSpec((2, 16, BAND), lambda n: (0, 0, n)))
        in_specs.append(pl.BlockSpec((halves, LANES, LANES), lambda n: (n, 0, 0)))
        args += [outer, edges]
    points = steps * BAND * len(spans) * LANES * count
    return pl.pallas_call(
        body,
        grid=(len(spans),),
        in_specs=in_specs,
        out_specs=out_specs,
        out_shape=out_shape,
        scratch_shapes=scratch,
        compiler_params=pltpu.CompilerParams(
            dimension_semantics=("arbitrary",), vmem_limit_bytes=56 * 1024 * 1024
        ),
        cost_estimate=pl.CostEstimate(flops=40 * points, bytes_accessed=2 * points, transcendentals=3 * points),
        name="march",
    )(*args)


def blend_kernel(tiles, order_ref, got_ref, out_ref):
    ranks = got_ref.shape[0]
    count = len(tiles)
    unroll = 4
    lower = lax.broadcasted_iota(jnp.int32, (8, LANES), 0) < 4
    zero = jnp.zeros((8, LANES), jnp.float32)
    one = zero + 1.0

    def layer(i, carry):
        carry = list(carry)
        for u in range(unroll):
            d = order_ref[i * unroll + u]
            for n in range(count):
                lanes = slice(LANES * n, LANES * n + LANES)
                red, green, blue, alpha, trans, high, low, half = carry[n]
                first = got_ref[d, 0:8, lanes]
                mixed = got_ref[d, 8:16, lanes]
                last = got_ref[d, 16:24, lanes]
                cover = decode(last & 0xFFFF) * trans
                red = red + trans * decode(lax.shift_right_logical(first, 16))
                green = green + trans * decode(first & 0xFFFF)
                blue = blue + trans * decode(lax.shift_right_logical(last, 16))
                alpha = alpha + cover
                trans = trans - cover
                level = decode(mixed & 0xFFFF)
                opaque = jnp.where(lower, pltpu.roll(level, 4, 0), level)
                high = high + half * decode(lax.shift_right_logical(mixed, 16))
                low = low + half * level
                half = half - half * opaque
                carry[n] = (red, green, blue, alpha, trans, high, low, half)
        return tuple(carry)

    start = tuple((zero, zero, zero, zero, one, zero, zero, one) for _ in range(count))
    final = lax.fori_loop(0, ranks // unroll, layer, start)
    for n in range(count):
        lanes = slice(LANES * tiles[n], LANES * tiles[n] + LANES)
        red, green, blue, alpha, _, high, low, _ = final[n]
        for r in range(8):
            for c, plane in enumerate((red, green, blue, alpha)):
                out_ref[c, r, :, lanes] = plane[r : r + 1]
        for r in range(4):
            for c, plane in enumerate((high, low)):
                out_ref[c, 8 + r, :, lanes] = plane[r : r + 1]
                out_ref[2 + c, 8 + r, :, lanes] = plane[4 + r : 5 + r]


def blend(tiles, order, got, image, width):
    ranks, rows, _ = got.shape
    whole = pl.BlockSpec(memory_space=pltpu.VMEM)
    scalars = pl.BlockSpec(memory_space=pltpu.SMEM)
    picture = jax.ShapeDtypeStruct((4, rows // 2, 1, width), jnp.float32)
    cost = pl.CostEstimate(flops=40 * got.size, bytes_accessed=4 * got.size, transcendentals=0)
    got = pltpu.with_memory_space_constraint(got, pltpu.VMEM)

    def early(place_ref, got_ref, out_ref, order_ref):
        def note(d, carry):
            order_ref[place_ref[d]] = d
            return carry

        lax.fori_loop(0, ranks, note, 0)
        blend_kernel(tiles, order_ref, got_ref, out_ref)

    def late(order_ref, got_ref, image_ref, out_ref):
        out_ref[...] = image_ref[...]
        blend_kernel(tiles, order_ref, got_ref, out_ref)

    if image is None:
        return pl.pallas_call(
            early,
            in_specs=[scalars, whole],
            out_specs=[whole, scalars],
            out_shape=[picture, jax.ShapeDtypeStruct((ranks,), jnp.int32)],
            cost_estimate=cost,
            name="blend",
        )(order, got)
    return pl.pallas_call(
        late, in_specs=[scalars, whole, whole], out_specs=whole, out_shape=picture, cost_estimate=cost, name="blend"
    )(order, got, image)


def on_device(volume, table_index, brick_position, tf_center, tf_width, tf_peak, tf_color):
    samples = volume[:, 0]
    cells = jnp.swapaxes(table_index[:, 0], 1, 2)
    steps, height, width = samples.shape
    ranks = lax.axis_size("depth")
    tables = [tf_center[None], tf_width[None], tf_peak[None], tf_color]
    tile_rank = lax.axis_index("tile")
    col_bit = tile_rank % 2
    row_bit = tile_rank // 2
    bands = height // BAND
    bare = [samples[:, n, :] for n in range(height) if 0 < n and n % BAND in (0, BAND - 1) and n < height - 1]
    pad = ((0, 0), (0, LANES - 2 * steps), (0, 0))
    send_row = jnp.where(row_bit == 0, samples[:, height - 1, :], samples[:, 0, :])
    inner_rows = jnp.pad(jnp.stack(bare[0:1] + bare[3:4], axis=1).reshape(1, 2 * steps, width), pad)
    got_row = from_partner(send_row, "tile", 1)
    *done, middle = march(CHUNKS[0], (1,), ranks, tables, samples, inner_rows, cells)
    zero_row = jnp.zeros_like(got_row)
    above = [jnp.where(row_bit == 1, got_row, zero_row), bare[1]]
    below = [bare[2], jnp.where(row_bit == 0, got_row, zero_row)]
    outer_rows = jnp.stack([jnp.stack(above, axis=1), jnp.stack(below, axis=1)], axis=0)
    outer_rows = jnp.pad(outer_rows.reshape(2, 2 * steps, width), pad)
    early, ends = march(CHUNKS[0], (0, bands - 1), ranks, tables, samples, outer_rows, cells, done=done)
    swap = functools.partial(lax.all_to_all, axis_name="depth", split_axis=0, concat_axis=0, tiled=True)
    got_early = swap(early)
    halves = BAND // LANES
    edges = jnp.concatenate([ends[:halves], middle, ends[halves:]], axis=0)
    marks = edges[:, : EDGES * steps].reshape(height // LANES, steps, EDGES, LANES)
    marks = jnp.where(col_bit == 0, marks[:, :, EDGES - 1], marks[:, :, 0])
    send_col = jnp.swapaxes(marks, 0, 1).reshape(steps, height).astype(jnp.bfloat16)
    got_col = jnp.pad(from_partner(send_col, "tile", 0).astype(jnp.float32), ((0, 16 - steps), (0, 0)))
    outer = jnp.stack([jnp.where(col_bit == 1, got_col, 0.0), jnp.where(col_bit == 0, got_col, 0.0)], axis=0)
    rows = jnp.concatenate([outer_rows[:1], inner_rows, outer_rows[1:]], axis=0)
    (late,) = march(CHUNKS[1], tuple(range(bands)), ranks, tables, samples, rows, cells, outer, edges)
    got_late = swap(late)
    image, order = blend(CHUNKS[0], brick_position, got_early, None, width)
    image = blend(CHUNKS[1], order, got_late, image, width)
    return jnp.swapaxes(image, 1, 2)


def solution(mesh):
    return jax.shard_map(
        on_device,
        mesh=mesh,
        in_specs=(
            P("depth", "tile", None, None),
            P("depth", "tile", None, None),
            P(),
            P(),
            P(),
            P(),
            P(),
        ),
        out_specs=P(None, "tile", "depth", None),
        check_vma=False,
    )
```

profile of v0, /device:TPU:8, one launch (start us, length us, event | category | flops | bytes accessed | tf_op | source)
XLA Modules:
  0.0 131.3 jit_solution(16462047504802591194)
XLA Ops:
  0.0 1.3 fusion.7
  1.3 3.1 %collective-permute-start = (bf16[12,512]{1,0:T(8,128)(2,1)S(1)}, bf16[12,512]{1,0:T(8,128)(2,1)S(1)}, u32[]{:S(2)}, u32[]{:S(2)}) collective-permute-start(bf16[12,512]{1,0:T(8,128)(2,1)S(1)} %bitcast.39), channel_id=1, source_target_pairs={{0,2},{1,3},{2,0},{3,1},{4,6},{5,7},{6,4},{7,5},{8,10},{9,11},{10,... | collective-permute-start | bytes 36872 | tf_op jit(solution)/shard_map/ppermute | solution.py:30
  4.4 0.1 pad_maximum_fusion.5
  4.5 0.7 pad.16.refs_5_
  5.1 5.7 %march.3 = (s32[1,256,128]{2,1,0:T(8,128)}, s32[1,256,128]{2,1,0:T(8,128)}, f32[2,128,128]{2,1,0:T(8,128)}) custom-call(f32[1,16]{1,0:T(1,128)} %bitcast.40, f32[1,16]{1,0:T(1,128)} %bitcast.43, f32[1,16]{1,0:T(1,128)} %bitcast.46, f32[3,16]{1,0:T(4,128)} %refs_3_.5, bf16[12,768,512]{2,1,0:T(8,128)(2,1)} %bitcast.29, bf16[1,128,512]{2,1,0:T(8,128)(2,1)} %pad.16.refs_5_, ...), custom_call_target="tpu_custom_call" | custom-call | flops 15728640 | bytes 786432 | tf_op jit(solution)/shard_map/march/pallas_call | solution.py:286
  10.8 0.0 collective-permute-done
  10.9 0.1 pad_maximum_fusion.3
  11.0 0.7 fusion.2.refs_5_
  11.7 0.0 copy-start.3
  11.7 9.2 %march.4 = (s32[64,24,128]{2,1,0:T(8,128)}, f32[4,128,128]{2,1,0:T(8,128)}) custom-call(f32[1,16]{1,0:T(1,128)} %bitcast.41, f32[1,16]{1,0:T(1,128)} %bitcast.44, f32[1,16]{1,0:T(1,128)} %bitcast.47, f32[3,16]{1,0:T(4,128)} %refs_3_.5, bf16[12,768,512]{2,1,0:T(8,128)(2,1)} %bitcast.30, bf16[2,128,512]{2,1,0:T(8,128)(2,1)} %fusion.2.refs_5_, ...), custom_call_target="tpu_custom_call" | custom-call | flops 31457280 | bytes 1572864 | tf_op jit(solution)/shard_map/march/pallas_call | solution.py:286
  20.9 0.0 copy-start
  20.9 0.0 copy-start.2
  20.9 12.2 %all-to-all-start = ((s32[64,24,128]{2,1,0:T(8,128)}), s32[64,24,128]{2,1,0:T(8,128)S(1)}, u32[]{:S(2)}, u32[]{:S(2)}) async-start(s32[64,24,128]{2,1,0:T(8,128)} %get-tuple-element.14), calls=%async_computation | async-start | bytes 1572864 | tf_op jit(solution)/shard_map/all_to_all | solution.py:404
  33.2 1.0 fusion.8
  34.2 0.0 copy-done.3
  34.2 0.0 copy-start.1
  34.2 0.1 fusion.10
  34.4 0.7 collective-permute-start.1
  35.1 0.0 copy-done
  35.1 0.0 copy-done.2
  35.1 0.8 pad_maximum_fusion.refs_7_
  35.9 2.4 %collective-permute-done.1 = bf16[12,768]{1,0:T(8,128)(2,1)S(1)} collective-permute-done((bf16[12,768]{1,0:T(8,128)(2,1)S(1)}, bf16[12,768]{1,0:T(8,128)(2,1)S(1)}, u32[]{:S(2)}, u32[]{:S(2)}) %collective-permute-start.1) | collective-permute-done | bytes 18464 | tf_op jit(solution)/shard_map/ppermute | solution.py:30
  38.3 0.6 pad_maximum_fusion.2.refs_9_
  38.9 0.0 copy-done.1
  38.9 22.2 %march.5 = s32[64,24,384]{2,1,0:T(8,128)} custom-call(f32[1,16]{1,0:T(1,128)} %bitcast.42, f32[1,16]{1,0:T(1,128)} %bitcast.45, f32[1,16]{1,0:T(1,128)} %bitcast.48, f32[3,16]{1,0:T(4,128)} %refs_3_.5, bf16[12,768,512]{2,1,0:T(8,128)(2,1)} %bitcast.31, bf16[12,768,512]{2,1,0:T(8,128)(2,1)} %bitcast.32, bf16[12,768,512]{2,1,0:T(8,128)(2,1)} %bitcast.33, ...), custom_call_target="tpu_custom_call" | custom-call | flops 141557760 | bytes 7077888 | tf_op jit(solution)/shard_map/march/pallas_call | solution.py:286
  61.2 0.0 all-to-all-done.got_ref
  61.2 10.3 %all-to-all-start.1 = ((s32[64,24,384]{2,1,0:T(8,128)}), s32[64,24,384]{2,1,0:T(8,128)S(1)}, u32[]{:S(2)}, u32[]{:S(2)}) async-start(s32[64,24,384]{2,1,0:T(8,128)} %march.5), calls=%async_computation.1 | async-start | bytes 4718592 | tf_op jit(solution)/shard_map/all_to_all | solution.py:414
  71.5 2.5 %blend.2 = (f32[4,12,1,512]{3,2,1,0:T(1,128)}, s32[64]{0:T(128)}) custom-call(s32[64]{0:T(128)} %place_ref.1, s32[64,24,128]{2,1,0:T(8,128)S(1)} %all-to-all-done.got_ref), custom_call_target="tpu_custom_call" | custom-call | flops 7864320 | bytes 786432 | tf_op jit(solution)/shard_map/blend/pallas_call | solution.py:368
  73.9 54.4 %all-to-all-done.1.got_ref = s32[64,24,384]{2,1,0:T(8,128)S(1)} async-done(((s32[64,24,384]{2,1,0:T(8,128)}), s32[64,24,384]{2,1,0:T(8,128)S(1)}, u32[]{:S(2)}, u32[]{:S(2)}) %all-to-all-start.1) | async-done | bytes 2359328 | tf_op jit(solution)/shard_map/all_to_all | solution.py:414
  128.3 3.0 %blend.3 = f32[4,12,1,512]{3,2,1,0:T(1,128)} custom-call(s32[64]{0:T(128)} %get-tuple-element.15.order_ref, s32[64,24,384]{2,1,0:T(8,128)S(1)} %all-to-all-done.1.got_ref, f32[4,12,1,512]{3,2,1,0:T(1,128)} %get-tuple-element.18.image_ref), custom_call_target="tpu_custom_call" | custom-call | flops 23592960 | bytes 2359296 | tf_op jit(solution)/shard_map/blend/pallas_call | solution.py:376
  (15 shorter events, 0.2 us)
Async XLA Ops:
  1.3 9.5 %collective-permute-start = (bf16[12,512]{1,0:T(8,128)(2,1)S(1)}, bf16[12,512]{1,0:T(8,128)(2,1)S(1)}, u32[]{:S(2)}, u32[]{:S(2)}) collective-permute-start(bf16[12,512]{1,0:T(8,128)(2,1)S(1)} %bitcast.39), channel_id=1, source_target_pairs={{0,2},{1,3},{2,0},{3,1},{4,6},{5,7},{6,4},{7,5},{8,10},{9,11},{10,... | collective-permute-start | bytes 36872 | tf_op jit(solution)/shard_map/ppermute | solution.py:30
  11.7 22.4 %copy-start.3 = (f32[2,128,128]{2,1,0:T(8,128)S(1)}, f32[2,128,128]{2,1,0:T(8,128)}, u32[]{:S(2)}) copy-start(f32[2,128,128]{2,1,0:T(8,128)} %get-tuple-element.17) | copy-start | bytes 393220
  20.9 14.1 %copy-start = (bf16[2,128,512]{2,1,0:T(8,128)(2,1)S(1)}, bf16[2,128,512]{2,1,0:T(8,128)(2,1)}, u32[]{:S(2)}) copy-start(bf16[2,128,512]{2,1,0:T(8,128)(2,1)} %fusion.2.refs_5_) | copy-start | bytes 786436
  20.9 14.2 %copy-start.2 = (bf16[1,128,512]{2,1,0:T(8,128)(2,1)S(1)}, bf16[1,128,512]{2,1,0:T(8,128)(2,1)}, u32[]{:S(2)}) copy-start(bf16[1,128,512]{2,1,0:T(8,128)(2,1)} %pad.16.refs_5_) | copy-start | bytes 393220
  20.9 40.2 %all-to-all-start = ((s32[64,24,128]{2,1,0:T(8,128)}), s32[64,24,128]{2,1,0:T(8,128)S(1)}, u32[]{:S(2)}, u32[]{:S(2)}) async-start(s32[64,24,128]{2,1,0:T(8,128)} %get-tuple-element.14), calls=%async_computation | async-start | bytes 1572864 | tf_op jit(solution)/shard_map/all_to_all | solution.py:404
  34.2 4.7 %copy-start.1 = (f32[6,128,128]{2,1,0:T(8,128)}, f32[6,128,128]{2,1,0:T(8,128)S(1)}, u32[]{:S(2)}) copy-start(f32[6,128,128]{2,1,0:T(8,128)S(1)} %pad_maximum_fusion.1.refs_10_) | copy-start | bytes 1179652
  34.4 3.9 %collective-permute-start.1 = (bf16[12,768]{1,0:T(8,128)(2,1)S(1)}, bf16[12,768]{1,0:T(8,128)(2,1)S(1)}, u32[]{:S(2)}, u32[]{:S(2)}) collective-permute-start(bf16[12,768]{1,0:T(8,128)(2,1)S(1)} %bitcast.38), channel_id=1, source_target_pairs={{0,1},{1,0},{2,3},{3,2},{4,5},{5,4},{6,7},{7,6},{8,9},{9,8},{10,11... | collective-permute-start | bytes 55304 | tf_op jit(solution)/shard_map/ppermute | solution.py:30
  61.2 67.2 %all-to-all-start.1 = ((s32[64,24,384]{2,1,0:T(8,128)}), s32[64,24,384]{2,1,0:T(8,128)S(1)}, u32[]{:S(2)}, u32[]{:S(2)}) async-start(s32[64,24,384]{2,1,0:T(8,128)} %march.5), calls=%async_computation.1 | async-start | bytes 4718592 | tf_op jit(solution)/shard_map/all_to_all | solution.py:414
where the time goes:
time: 132 us; the launch traced here: 131 us
  waiting for transfers between devices  56.8 us (43%)
  Pallas kernels  42.5 us (32%)
  starting transfers between devices  26.3 us (20%)
  other arithmetic  3.63 us (3%)
  local copies, waits for them, and re-layouts  1.87 us (1%)
    all_to_all x1, waiting for transfers between devices, on_device(): got_late = swap(late)  54.4 us
    pallas_call x3, Pallas kernels, march(): pl.pallas_call(body, grid=(len(spans),), in_specs=in_specs, out_specs=out...  37 us
    all_to_all x1, starting transfers between devices, on_device(): got_early = swap(early)  12.2 us
    all_to_all x1, starting transfers between devices, on_device(): got_late = swap(late)  10.3 us
    ppermute x2, starting transfers between devices, from_partner(): lax.ppermute(value, axis, [(i, i ^ 1 << apart) for i in range(lax.axis_si...  3.79 us
    pallas_call x1, Pallas kernels, blend(): pl.pallas_call(late, in_specs=[scalars, whole, whole], out_specs=whole, o...  2.97 us
  transfers between devices with their start and end apart: 4, of which 2 were waited for; matrix products, arithmetic and copies ran while one was open for 3% of the time, Pallas kernels for 23%

commit v1 on v0

--- a/solution.py
+++ b/solution.py
@@ -15,7 +15,7 @@
 LOG2E = 1.4426950408889634
 LEVELS = 65535.0
 SCALE = LEVELS**4
-CHUNKS = ((1,), (0, 2, 3))
+CHUNKS = ((1, 2), (0, 3))
 EDGES = 8
 STRIP = 4
 LIGHT = 32
@@ -199,8 +199,8 @@
         piece = height // out_ref.shape[0]
 
         def pack(d, carry):
-            for u in range(4):
-                e = d * 4 + u
+            for u in range(8):
+                e = d * 8 + u
                 r = e * piece
                 for k in range(count):
                     lanes = slice(LANES * k, LANES * k + LANES)
@@ -210,7 +210,7 @@
                     out_ref[e, 16:24, lanes] = turn_b[k, pl.ds(r, 8), :]
             return carry
 
-        lax.fori_loop(0, out_ref.shape[0] // 4, pack, 0)
+        lax.fori_loop(0, out_ref.shape[0] // 8, pack, 0)
 
 
 def march(tiles, spans, ranks, tables, samples, rim_rows, cells, outer=None, edges=None, done=None):
@@ -301,7 +301,7 @@
 def blend_kernel(tiles, order_ref, got_ref, out_ref):
     ranks = got_ref.shape[0]
     count = len(tiles)
-    unroll = 4
+    unroll = 8
     lower = lax.broadcasted_iota(jnp.int32, (8, LANES), 0) < 4
     zero = jnp.zeros((8, LANES), jnp.float32)
     one = zero + 1.0

time: 132 us -> 128 us (0.970)
  the two profiles are of different devices: /device:TPU:8 before, /device:TPU:1 now
where the time goes in v1:
time: 128 us; the launch traced here: 127 us
  waiting for transfers between devices  56.7 us (44%)
  Pallas kernels  42.5 us (33%)
  starting transfers between devices  23.2 us (18%)
  other arithmetic  3.64 us (3%)
    pallas_call x3, Pallas kernels, march(): pl.pallas_call(body, grid=(len(spans),), in_specs=in_specs, out_specs=out...  37.2 us
    all_to_all x1, waiting for transfers between devices, on_device(): got_late = swap(late)  36.2 us
    all_to_all x1, waiting for transfers between devices, on_device(): got_early = swap(early)  18.9 us
    all_to_all x1, starting transfers between devices, on_device(): got_early = swap(early)  12.8 us
    all_to_all x1, starting transfers between devices, on_device(): got_late = swap(late)  6.38 us
    ppermute x2, starting transfers between devices, from_partner(): lax.ppermute(value, axis, [(i, i ^ 1 << apart) for i in range(lax.axis_si...  4.04 us
    pallas_call x1, Pallas kernels, blend(): pl.pallas_call(early, in_specs=[scalars, whole], out_specs=[whole, scalar...  2.82 us
  transfers between devices with their start and end apart: 4, of which 3 were waited for; matrix products, arithmetic and copies ran while one was open for 2% of the time, Pallas kernels for 21%

profile of v1, /device:TPU:1, one launch (start us, length us, event | category | flops | bytes accessed | tf_op | source)
XLA Modules:
  0.0 127.4 jit_solution(12566522980255475829)
XLA Ops:
  0.0 1.3 fusion.7
  1.3 3.6 %collective-permute-start = (bf16[12,512]{1,0:T(8,128)(2,1)S(1)}, bf16[12,512]{1,0:T(8,128)(2,1)S(1)}, u32[]{:S(2)}, u32[]{:S(2)}) collective-permute-start(bf16[12,512]{1,0:T(8,128)(2,1)S(1)} %bitcast.38), channel_id=1, source_target_pairs={{0,2},{1,3},{2,0},{3,1},{4,6},{5,7},{6,4},{7,5},{8,10},{9,11},{10,... | collective-permute-start | bytes 36872 | tf_op jit(solution)/shard_map/ppermute | solution.py:30
  4.9 0.1 pad_maximum_fusion.5
  5.0 0.7 pad.16.refs_5_
  5.7 7.7 %march.3 = (s32[2,256,128]{2,1,0:T(8,128)}, s32[2,256,128]{2,1,0:T(8,128)}, f32[2,128,128]{2,1,0:T(8,128)}) custom-call(f32[1,16]{1,0:T(1,128)} %bitcast.39, f32[1,16]{1,0:T(1,128)} %bitcast.42, f32[1,16]{1,0:T(1,128)} %bitcast.45, f32[3,16]{1,0:T(4,128)} %refs_3_.5, bf16[12,768,512]{2,1,0:T(8,128)(2,1)} %bitcast.29, bf16[1,128,512]{2,1,0:T(8,128)(2,1)} %pad.16.refs_5_, ...), custom_call_target="tpu_custom_call" | custom-call | flops 31457280 | bytes 1572864 | tf_op jit(solution)/shard_map/march/pallas_call | solution.py:286
  13.4 0.0 collective-permute-done
  13.4 0.1 pad_maximum_fusion.3
  13.6 0.7 fusion.2.refs_5_
  14.3 13.4 %march.4 = (s32[64,24,256]{2,1,0:T(8,128)}, f32[4,128,128]{2,1,0:T(8,128)}) custom-call(f32[1,16]{1,0:T(1,128)} %bitcast.40, f32[1,16]{1,0:T(1,128)} %bitcast.43, f32[1,16]{1,0:T(1,128)} %bitcast.46, f32[3,16]{1,0:T(4,128)} %refs_3_.5, bf16[12,768,512]{2,1,0:T(8,128)(2,1)} %bitcast.30, bf16[2,128,512]{2,1,0:T(8,128)(2,1)} %fusion.2.refs_5_, ...), custom_call_target="tpu_custom_call" | custom-call | flops 62914560 | bytes 3145728 | tf_op jit(solution)/shard_map/march/pallas_call | solution.py:286
  27.7 0.0 copy-start.3
  27.7 0.0 copy-start.4
  27.7 12.8 %all-to-all-start = ((s32[64,24,256]{2,1,0:T(8,128)}), s32[64,24,256]{2,1,0:T(8,128)S(1)}, u32[]{:S(2)}, u32[]{:S(2)}) async-start(s32[64,24,256]{2,1,0:T(8,128)} %get-tuple-element.14), calls=%async_computation | async-start | bytes 3145728 | tf_op jit(solution)/shard_map/all_to_all | solution.py:404
  40.5 0.0 copy-start
  40.5 0.0 copy-start.2
  40.5 0.0 copy-done.3
  40.6 0.0 copy-done.4
  40.6 0.0 copy-start.1
  40.6 0.1 fusion.10
  40.8 0.4 collective-permute-start.1
  41.2 0.3 copy-done
  41.5 0.0 copy-done.2
  41.5 0.8 pad_maximum_fusion.refs_6_
  42.3 1.5 %collective-permute-done.1 = bf16[12,768]{1,0:T(8,128)(2,1)S(1)} collective-permute-done((bf16[12,768]{1,0:T(8,128)(2,1)S(1)}, bf16[12,768]{1,0:T(8,128)(2,1)S(1)}, u32[]{:S(2)}, u32[]{:S(2)}) %collective-permute-start.1) | collective-permute-done | bytes 18464 | tf_op jit(solution)/shard_map/ppermute | solution.py:30
  43.8 0.6 pad_maximum_fusion.2.refs_8_
  44.5 0.0 copy-done.1
  44.5 16.1 %march.5 = s32[64,24,256]{2,1,0:T(8,128)} custom-call(f32[1,16]{1,0:T(1,128)} %bitcast.41, f32[1,16]{1,0:T(1,128)} %bitcast.44, f32[1,16]{1,0:T(1,128)} %bitcast.47, f32[3,16]{1,0:T(4,128)} %refs_3_.5, bf16[12,768,512]{2,1,0:T(8,128)(2,1)} %bitcast.31, bf16[12,768,512]{2,1,0:T(8,128)(2,1)} %bitcast.32, bf16[3,128,512]{2,1,0:T(8,128)(2,1)} %pad_maximum_fusion.refs_6_, ...), custom_call_target="tpu_custom_call" | custom-call | flops 94371840 | bytes 4718592 | tf_op jit(solution)/shard_map/march/pallas_call | solution.py:286
  60.6 18.9 %all-to-all-done.got_ref = s32[64,24,256]{2,1,0:T(8,128)S(1)} async-done(((s32[64,24,256]{2,1,0:T(8,128)}), s32[64,24,256]{2,1,0:T(8,128)S(1)}, u32[]{:S(2)}, u32[]{:S(2)}) %all-to-all-start) | async-done | bytes 1572896 | tf_op jit(solution)/shard_map/all_to_all | solution.py:404
  79.5 6.4 %all-to-all-start.1 = ((s32[64,24,256]{2,1,0:T(8,128)}), s32[64,24,256]{2,1,0:T(8,128)S(1)}, u32[]{:S(2)}, u32[]{:S(2)}) async-start(s32[64,24,256]{2,1,0:T(8,128)} %march.5), calls=%async_computation.1 | async-start | bytes 3145728 | tf_op jit(solution)/shard_map/all_to_all | solution.py:414
  85.9 2.8 %blend.2 = (f32[4,12,1,512]{3,2,1,0:T(1,128)}, s32[64]{0:T(128)}) custom-call(s32[64]{0:T(128)} %place_ref.1, s32[64,24,256]{2,1,0:T(8,128)S(1)} %all-to-all-done.got_ref), custom_call_target="tpu_custom_call" | custom-call | flops 15728640 | bytes 1572864 | tf_op jit(solution)/shard_map/blend/pallas_call | solution.py:368
  88.8 36.2 %all-to-all-done.1.got_ref = s32[64,24,256]{2,1,0:T(8,128)S(1)} async-done(((s32[64,24,256]{2,1,0:T(8,128)}), s32[64,24,256]{2,1,0:T(8,128)S(1)}, u32[]{:S(2)}, u32[]{:S(2)}) %all-to-all-start.1) | async-done | bytes 1572896 | tf_op jit(solution)/shard_map/all_to_all | solution.py:414
  125.0 2.5 %blend.3 = f32[4,12,1,512]{3,2,1,0:T(1,128)} custom-call(s32[64]{0:T(128)} %get-tuple-element.15.order_ref, s32[64,24,256]{2,1,0:T(8,128)S(1)} %all-to-all-done.1.got_ref, f32[4,12,1,512]{3,2,1,0:T(1,128)} %get-tuple-element.18.image_ref), custom_call_target="tpu_custom_call" | custom-call | flops 15728640 | bytes 1572864 | tf_op jit(solution)/shard_map/blend/pallas_call | solution.py:376
  (16 shorter events, 0.2 us)
Async XLA Ops:
  1.3 12.1 %collective-permute-start = (bf16[12,512]{1,0:T(8,128)(2,1)S(1)}, bf16[12,512]{1,0:T(8,128)(2,1)S(1)}, u32[]{:S(2)}, u32[]{:S(2)}) collective-permute-start(bf16[12,512]{1,0:T(8,128)(2,1)S(1)} %bitcast.38), channel_id=1, source_target_pairs={{0,2},{1,3},{2,0},{3,1},{4,6},{5,7},{6,4},{7,5},{8,10},{9,11},{10,... | collective-permute-start | bytes 36872 | tf_op jit(solution)/shard_map/ppermute | solution.py:30
  27.7 12.8 %copy-start.3 = (f32[4,128,128]{2,1,0:T(8,128)S(1)}, f32[4,128,128]{2,1,0:T(8,128)}, u32[]{:S(2)}) copy-start(f32[4,128,128]{2,1,0:T(8,128)} %get-tuple-element.16) | copy-start | bytes 786436
  27.7 12.8 %copy-start.4 = (f32[2,128,128]{2,1,0:T(8,128)S(1)}, f32[2,128,128]{2,1,0:T(8,128)}, u32[]{:S(2)}) copy-start(f32[2,128,128]{2,1,0:T(8,128)} %get-tuple-element.17) | copy-start | bytes 393220
  27.7 51.8 %all-to-all-start = ((s32[64,24,256]{2,1,0:T(8,128)}), s32[64,24,256]{2,1,0:T(8,128)S(1)}, u32[]{:S(2)}, u32[]{:S(2)}) async-start(s32[64,24,256]{2,1,0:T(8,128)} %get-tuple-element.14), calls=%async_computation | async-start | bytes 3145728 | tf_op jit(solution)/shard_map/all_to_all | solution.py:404
  40.5 1.0 copy-start
  40.5 1.0 copy-start.2
  40.6 3.9 %copy-start.1 = (f32[6,128,128]{2,1,0:T(8,128)}, f32[6,128,128]{2,1,0:T(8,128)S(1)}, u32[]{:S(2)}) copy-start(f32[6,128,128]{2,1,0:T(8,128)S(1)} %pad_maximum_fusion.1.refs_9_) | copy-start | bytes 1179652
  40.8 3.1 %collective-permute-start.1 = (bf16[12,768]{1,0:T(8,128)(2,1)S(1)}, bf16[12,768]{1,0:T(8,128)(2,1)S(1)}, u32[]{:S(2)}, u32[]{:S(2)}) collective-permute-start(bf16[12,768]{1,0:T(8,128)(2,1)S(1)} %bitcast.37), channel_id=1, source_target_pairs={{0,1},{1,0},{2,3},{3,2},{4,5},{5,4},{6,7},{7,6},{8,9},{9,8},{10,11... | collective-permute-start | bytes 55304 | tf_op jit(solution)/shard_map/ppermute | solution.py:30
  79.5 45.4 %all-to-all-start.1 = ((s32[64,24,256]{2,1,0:T(8,128)}), s32[64,24,256]{2,1,0:T(8,128)S(1)}, u32[]{:S(2)}, u32[]{:S(2)}) async-start(s32[64,24,256]{2,1,0:T(8,128)} %march.5), calls=%async_computation.1 | async-start | bytes 3145728 | tf_op jit(solution)/shard_map/all_to_all | solution.py:414
